TPU v7x, 32 devices: a whole 2x2x4 slice. The times are simulated.
32 devices in a mesh: row: 8 (over y, x, core), col: 4 (over z).
Axes of the slice: x: 2, y: 2, z: 4, core: 2. Of those that a mesh axis runs over, the one named last changes fastest.
Arguments:
- legendre: bfloat16 [4, 128, 89, 8, 128], P(None, 'col', None, 'row'), may hold values from -6 to 6
- longitude: float32 [512], replicated, may hold values from -3.140625 to 3.140625
- obs_weight: float32 [512], replicated, may hold values from 0.1 to 1.9
- span_weight: float32 [8], replicated, may hold values from 0.3 to 3
- span_of: int32 [512], replicated, may hold values from 0 to 7
- tile_order: int32 [712], replicated, may hold values from 0 to 711, each once
- slab_start: int32 [1], replicated, may hold values from 0 to 704
- resident: float32 [89, 8, 4, 128, 128], P(None, 'row', 'col'), may hold values from -6 to 6
Outputs:
- updated: float32 [89, 8, 4, 128, 128], P(None, 'row', 'col')
Inputs may be any that keep to these rules, and one draw needn't show every extreme that they name: tile_order is a permutation of the slot positions.
All inputs are finite; a program needn't handle non-finite values.
Results may differ from a plain program's by a relative error of at most 0.00074.
Values may be sent and summed in bfloat16 or wider, within the bound.
No kernel may reach another device: no remote copies, remote signals or barrier semaphores. Data moves between devices by JAX's collectives and lax.ppermute only.
A program may use at most 64 MiB of HBM per device.

v0:
```python
import math
import jax
import jax.numpy as jnp
from jax import lax
from jax.sharding import PartitionSpec as P

DEGREE = 300
UNK = 90600


def lookup_weights(obs_weight, span_weight, span_of):
    group_count = span_weight.shape[0]
    matches = span_of[:, None] == jnp.arange(group_count, dtype=jnp.int32)[None, :]
    factor = jnp.sum(jnp.where(matches, span_weight[None, :], 0.0), axis=1)
    return obs_weight * factor * (0.25 / math.sqrt(obs_weight.shape[0]))


def locate(tile_order, targets):
    places = jnp.arange(tile_order.shape[0], dtype=jnp.int32)
    return jnp.sum(jnp.where(tile_order[None, :] == targets[:, None], places[None, :], 0), axis=1)


def contract_rows(left_side, right_side):
    return lax.dot_general(
        left_side, right_side, (((0,), (0,)), ((), ())), preferred_element_type=jnp.float32
    )


def per_device(
    legendre, longitude, obs_weight, span_weight, span_of, tile_order, slab_start, resident
):
    block_count, shard_rows, slot_count, _, tile_size = legendre.shape
    row_count = lax.axis_size("row")
    col_count = lax.axis_size("col")
    row_index = lax.axis_index("row")
    col_index = lax.axis_index("col")
    block_rows = shard_rows * col_count
    order_map = tile_order.reshape(slot_count, row_count)
    own_tiles = lax.dynamic_slice_in_dim(order_map, row_index, 1, 1)[:, 0]
    unknown = own_tiles[:, None] * tile_size + jnp.arange(tile_size, dtype=jnp.int32)[None, :]
    orders = (unknown % (DEGREE + 1)).astype(jnp.float32).reshape(1, slot_count * tile_size)
    is_valid = (unknown < UNK).reshape(1, slot_count * tile_size)
    targets = slab_start[0] + jnp.arange(col_count, dtype=jnp.int32)
    positions = locate(tile_order, targets)
    target = targets[col_index]
    root_row = positions[col_index] % row_count
    root_slots = positions // row_count
    root_slot = root_slots[col_index]
    is_root = row_index == root_row
    weights = lookup_weights(obs_weight, span_weight, span_of).reshape(block_count, block_rows)
    angles = longitude.reshape(block_count, block_rows)
    in_lower = own_tiles >= target
    zero_piece = jnp.zeros((), jnp.bfloat16)
    all_values = legendre.reshape(block_count * shard_rows, slot_count * tile_size)
    own_angles = lax.dynamic_slice_in_dim(angles, col_index * shard_rows, shard_rows, 1)
    own_angles = own_angles.reshape(block_count * shard_rows)
    design_all = jnp.where(
        is_valid, all_values.astype(jnp.float32) * jnp.cos(own_angles[:, None] * orders), 0.0
    ).astype(jnp.bfloat16)
    design_all = design_all.reshape(block_count, shard_rows, slot_count * tile_size)
    gathered = lax.all_gather(design_all, "col", axis=1, tiled=True)
    gathered = gathered.reshape(block_count * block_rows, slot_count * tile_size)
    candidate = lax.dynamic_slice_in_dim(gathered, root_slot * tile_size, tile_size, 1)
    column = lax.psum(jnp.where(is_root, candidate, zero_piece), "row").astype(jnp.float32)
    weighted = (weights.reshape(block_count * block_rows)[:, None] * column).astype(jnp.bfloat16)
    running = contract_rows(gathered, weighted)
    update = jnp.where(
        in_lower[:, None, None], running.reshape(slot_count, tile_size, tile_size), 0.0
    )
    return resident + update.reshape(resident.shape)


def solution(mesh):
    placed = (
        P(None, "col", None, "row", None),
        P(),
        P(),
        P(),
        P(),
        P(),
        P(),
        P(None, "row", "col", None, None),
    )
    return jax.shard_map(
        per_device,
        mesh=mesh,
        in_specs=placed,
        out_specs=P(None, "row", "col", None, None),
        check_vma=False,
    )
```

profile of v0, /device:TPU:0, one launch (start us, length us, event | category | flops | bytes accessed | tf_op | source)
XLA Modules:
  0.0 322.1 jit_solution(3542823524447298766)
XLA Ops:
  6.5 0.0 copy-start
  6.5 0.0 all-gather.2.cloned.1.call-start
  6.5 0.8 reshape.90
  7.3 0.2 multiply_reduce_fusion
  7.5 0.1 fusion.4
  7.6 0.1 fusion.8
  7.7 5.5 %copy.20 = f32[4,32,89,1,128]{4,2,1,0,3:T(8,128)} copy(bf16[4,32,89,1,128]{4,1,3,2,0:T(8,128)(2,1)} %param.8) | data formatting | bytes 8749056 | tf_op jit(solution)/shard_map/convert_element_type | solution.py:58
  13.2 7.2 %reshape.94 = f32[4,32,11392]{2,1,0:T(8,128)} reshape(f32[4,32,89,1,128]{4,2,1,0,3:T(8,128)} %copy.20) | data formatting | bytes 11665408 | tf_op jit(solution)/shard_map/convert_element_type | solution.py:58
  20.4 0.1 constant_dynamic-slice_fusion
  20.5 22.0 %select_convert_fusion = bf16[4,32,11392]{2,1,0:T(8,128)(2,1)} fusion(f32[4,32,11392]{2,1,0:T(8,128)} %reshape.94, f32[11392]{0:T(1024)S(1)} %fusion.4, f32[4,32]{1,0:T(4,128)S(1)} %constant_dynamic-slice_fusion, pred[11392]{0:T(1024)(128)(4,1)S(1)} %fusion.8), kind=kLoop, calls=%fused_computation.2 | loop fusion | flops 5832704 | bytes 8806528 | tf_op jit(solution)/shard_map/convert_element_type | solution.py:59
  42.6 0.0 all-gather.2.cloned.1.call-update
  42.6 0.0 all-reduce.2.cloned.1.call-start
  43.3 0.2 select_reduce_fusion.1
  43.5 0.6 dynamic_slice.21
  46.0 0.6 dynamic_slice.22
  47.3 0.1 select_reduce_fusion
  47.4 201.2 %all-gather.2.cloned.1.call-done = bf16[4,128,11392]{2,1,0:T(8,128)(2,1)} async-done(((bf16[4,32,11392]{2,1,0:T(8,128)(2,1)}), bf16[4,128,11392]{2,1,0:T(8,128)(2,1)}) %all-gather.2.cloned.1.call-update) | async-done | bytes 11665424 | tf_op jit(solution)/shard_map/all_gather | solution.py:61
  248.6 1.6 dynamic-slice_select_fusion
  250.2 0.0 all-reduce.2.cloned.1.call-update
  250.3 0.6 dynamic_slice.19
  250.9 0.8 compare_reduce_fusion
  251.7 16.2 %copy.21 = bf16[11392,512]{1,0:T(8,128)(2,1)} copy(bf16[11392,512]{0,1:T(8,128)(2,1)} %bitcast.39) | data formatting | bytes 23330816 | tf_op jit(solution)/shard_map/dot_general | solution.py:24
  267.9 35.4 %all-reduce.2.cloned.1.call-done = bf16[512,128]{1,0:T(8,128)(2,1)} async-done(((bf16[512,128]{1,0:T(8,128)(2,1)}), bf16[512,128]{1,0:T(8,128)(2,1)}) %all-reduce.2.cloned.1.call-update) | async-done | bytes 131088 | tf_op jit(solution)/shard_map/psum | solution.py:64
  303.3 11.9 %fusion = f32[89,1,1,128,128]{4,3,2,1,0:T(8,128)} fusion(f32[89,1,1,128,128]{4,3,2,1,0:T(8,128)} %param.15, pred[89]{0:T(512)(128)(4,1)S(1)} %compare_reduce_fusion, bf16[89,128,512]{2,1,0:T(8,128)(2,1)} %bitcast.37, bf16[512,128]{1,0:T(8,128)(2,1)} %all-reduce.2.cloned.1.call-done, f32[512]{0:T(512)S(1)} %multiply_multiply_fusion), kind=kOutput, calls=%fused_computation.1 | convolution fusion | flops 1496285184 | bytes 23464024 | tf_op jit(solution)/shard_map/dot_general | solution.py:24
  (12 shorter events, 0.0 us)
Async XLA Ops:
  6.5 13.9 %copy-start = (f32[512]{0:T(512)S(1)}, f32[512]{0:T(512)}, u32[]{:S(2)}) copy-start(f32[512]{0:T(512)} %param.9) | copy-start | bytes 6148
  6.5 242.1 %all-gather.2.cloned.1.call-start = ((), (), s32[]{:S(2)}) async-start(), calls=%async_computation | async-start | bytes 14581760 | tf_op jit(solution)/shard_map/all_gather | solution.py:61
  20.5 22.8 %copy-start.1 = (s32[712]{0:T(1024)S(1)}, s32[712]{0:T(1024)}, u32[]{:S(2)}) copy-start(s32[712]{0:T(1024)} %param.13) | copy-start | bytes 8548
  20.5 26.8 %copy-start.3 = (s32[512]{0:T(512)S(1)}, s32[512]{0:T(512)}, u32[]{:S(2)}) copy-start(s32[512]{0:T(512)} %param.12) | copy-start | bytes 6148
  20.5 26.8 %copy-start.4 = (f32[8]{0:T(128)S(1)}, f32[8]{0:T(128)}, u32[]{:S(2)}) copy-start(f32[8]{0:T(128)} %param.11) | copy-start | bytes 100
  20.5 229.8 %copy-start.2 = (f32[512]{0:T(512)S(1)}, f32[512]{0:T(512)}, u32[]{:S(2)}) copy-start(f32[512]{0:T(512)} %param.10) | copy-start | bytes 6148
  42.6 260.7 %all-reduce.2.cloned.1.call-start = ((), (), s32[]{:S(2)}) async-start(), calls=%async_computation.1 | async-start | bytes 262144 | tf_op jit(solution)/shard_map/psum | solution.py:64
Sparse Core Ops, SparseCore 0:
  42.7 205.8 all-gather.1
  251.7 51.6 all-reduce.1
where the time goes:
time: 323 us; the launch traced here: 322 us
  waiting for transfers between devices  237 us (73%)
  local copies, waits for them, and re-layouts  31.5 us (10%)
  other arithmetic  25.1 us (8%)
  between operations  16.8 us (5%)
  matrix products  11.9 us (4%)
    all_gather x1, waiting for transfers between devices, per_device(): gathered = lax.all_gather(design_all, 'col', axis=1, tiled=True)  201 us
    psum x1, waiting for transfers between devices, per_device(): lax.psum(jnp.where(is_root, candidate, zero_piece), 'row')  35.4 us
    convert_element_type x1, other arithmetic, per_device(): design_all = jnp.where(is_valid, all_values.astype(jnp.float32) * jnp.cos...  22 us
    dot_general x1, local copies, waits for them, and re-layouts, contract_rows(): lax.dot_general(left_side, right_side, (((0,), (0,)), ((), ())), preferre...  16.2 us
    convert_element_type x2, local copies, waits for them, and re-layouts, per_device(): all_values.astype(jnp.float32) * jnp.cos(own_angles[:, None] * orders)  12.7 us
    dot_general x1, matrix products, contract_rows(): lax.dot_general(left_side, right_side, (((0,), (0,)), ((), ())), preferre...  11.9 us
  transfers between devices with their start and end apart: 2, of which 2 were waited for; matrix products, arithmetic and copies ran while one was open for 6% of the time, Pallas kernels for 0%

commit v1 on v0

--- a/solution.py
+++ b/solution.py
@@ -58,7 +58,13 @@
         is_valid, all_values.astype(jnp.float32) * jnp.cos(own_angles[:, None] * orders), 0.0
     ).astype(jnp.bfloat16)
     design_all = design_all.reshape(block_count, shard_rows, slot_count * tile_size)
-    gathered = lax.all_gather(design_all, "col", axis=1, tiled=True)
+    count = lax.axis_size("col")
+    held, blocks = (design_all, [design_all])
+    for _ in range(count - 1):
+        held = lax.ppermute(held, "col", [(i, (i + 1) % count) for i in range(count)])
+        blocks.insert(0, held)
+    line = jnp.concatenate(blocks, axis=1)
+    gathered = jnp.roll(line, (lax.axis_index("col") + 1) * design_all.shape[1], axis=1)
     gathered = gathered.reshape(block_count * block_rows, slot_count * tile_size)
     candidate = lax.dynamic_slice_in_dim(gathered, root_slot * tile_size, tile_size, 1)
     column = lax.psum(jnp.where(is_root, candidate, zero_piece), "row").astype(jnp.float32)

time: 323 us -> 368 us (1.14)
  other arithmetic: 25.1 us -> 62.4 us
  local copies, waits for them, and re-layouts: 31.5 us -> 46.6 us
  waiting for transfers between devices: 237 us -> 226 us
    all_gather x1 -> x0, waiting for transfers between devices: 201 us -> none  [per_device(): gathered = lax.all_gather(design_all, 'col', axis=1, tiled=True)]
    ppermute x0 -> x3, waiting for transfers between devices: none -> 193 us  [per_device(): lax.ppermute(held, 'col', [(i, (i + 1) % count) for i in range(count)])]
    unnamed x0 -> x2, other arithmetic: none -> 19.6 us
    concatenate x0 -> x1, other arithmetic: none -> 19.4 us  [per_device(): jnp.roll(line, (lax.axis_index('col') + 1) * design_all.shape[1], axis=1)]
    unnamed x10 -> x24, local copies, waits for them, and re-layouts: 0.02 us -> 14.2 us
  transfers between devices with their start and end apart: 2 -> 4, of which waited for: 2 -> 4; matrix products, arithmetic and copies ran while one was open for 6% -> 5% of each run, Pallas kernels for 0% -> 0%
where the time goes in v1:
time: 368 us; the launch traced here: 367 us
  waiting for transfers between devices  226 us (61%)
  other arithmetic  62.4 us (17%)
  local copies, waits for them, and re-layouts  46.6 us (13%)
  between operations  16.6 us (5%)
  matrix products  11.9 us (3%)
    ppermute x3, waiting for transfers between devices, per_device(): lax.ppermute(held, 'col', [(i, (i + 1) % count) for i in range(count)])  193 us
    psum x1, waiting for transfers between devices, per_device(): lax.psum(jnp.where(is_root, candidate, zero_piece), 'row')  33.7 us
    convert_element_type x1, other arithmetic, per_device(): design_all = jnp.where(is_valid, all_values.astype(jnp.float32) * jnp.cos...  21.2 us
    unnamed x2, other arithmetic  19.6 us
    concatenate x1, other arithmetic, per_device(): jnp.roll(line, (lax.axis_index('col') + 1) * design_all.shape[1], axis=1)  19.4 us
    dot_general x1, local copies, waits for them, and re-layouts, contract_rows(): lax.dot_general(left_side, right_side, (((0,), (0,)), ((), ())), preferre...  16.2 us
    unnamed x24, local copies, waits for them, and re-layouts  14.2 us
    convert_element_type x2, local copies, waits for them, and re-layouts, per_device(): all_values.astype(jnp.float32) * jnp.cos(own_angles[:, None] * orders)  12.7 us
  transfers between devices with their start and end apart: 4, of which 4 were waited for; matrix products, arithmetic and copies ran while one was open for 5% of the time, Pallas kernels for 0%

profile of v1, /device:TPU:0, one launch (start us, length us, event | category | flops | bytes accessed | tf_op | source)
XLA Modules:
  0.0 367.0 jit_solution(6194400505150147449)
XLA Ops:
  6.5 0.8 reshape.90
  7.7 5.5 %copy.20 = f32[4,32,89,1,128]{4,2,1,0,3:T(8,128)} copy(bf16[4,32,89,1,128]{4,1,3,2,0:T(8,128)(2,1)} %param.8) | data formatting | bytes 8749056 | tf_op jit(solution)/shard_map/convert_element_type | solution.py:58
  13.2 7.2 %reshape.94 = f32[4,32,11392]{2,1,0:T(8,128)} reshape(f32[4,32,89,1,128]{4,2,1,0,3:T(8,128)} %copy.20) | data formatting | bytes 11665408 | tf_op jit(solution)/shard_map/convert_element_type | solution.py:58
  20.5 21.2 %select_convert_fusion = bf16[4,32,11392]{2,1,0:T(8,128)(2,1)S(1)} fusion(f32[4,32,11392]{2,1,0:T(8,128)} %reshape.94, f32[11392]{0:T(1024)S(1)} %fusion.4, f32[4,32]{1,0:T(4,128)S(1)} %constant_dynamic-slice_fusion.1, pred[11392]{0:T(1024)(128)(4,1)S(1)} %fusion.8), kind=kLoop, calls=%fused_computation.2 | loop fusion | flops 5832704 | bytes 8806528 | tf_op jit(solution)/shard_map/convert_element_type | solution.py:59
  41.7 3.1 collective-permute-start
  44.8 65.2 %collective-permute-done = bf16[4,32,11392]{2,1,0:T(8,128)(2,1)S(1)} collective-permute-done((bf16[4,32,11392]{2,1,0:T(8,128)(2,1)S(1)}, bf16[4,32,11392]{2,1,0:T(8,128)(2,1)S(1)}, u32[]{:S(2)}, u32[]{:S(2)}) %collective-permute-start) | collective-permute-done | bytes 2916384 | tf_op jit(solution)/shard_map/ppermute | solution.py:64
  110.1 66.2 %collective-permute-done.1 = bf16[4,32,11392]{2,1,0:T(8,128)(2,1)} collective-permute-done((bf16[4,32,11392]{2,1,0:T(8,128)(2,1)S(1)}, bf16[4,32,11392]{2,1,0:T(8,128)(2,1)}, u32[]{:S(2)}, u32[]{:S(2)}) %collective-permute-start.1) | collective-permute-done | bytes 2916384 | tf_op jit(solution)/shard_map/ppermute | solution.py:64
  177.2 0.6 dynamic_slice.26
  179.5 0.6 dynamic_slice.27
  180.8 61.1 %collective-permute-done.2 = bf16[4,32,11392]{2,1,0:T(8,128)(2,1)} collective-permute-done((bf16[4,32,11392]{2,1,0:T(8,128)(2,1)}, bf16[4,32,11392]{2,1,0:T(8,128)(2,1)}, u32[]{:S(2)}, u32[]{:S(2)}) %collective-permute-start.2) | collective-permute-done | bytes 2916384 | tf_op jit(solution)/shard_map/ppermute | solution.py:64
  241.9 2.3 constant_dynamic-update-slice_fusion.7
  244.2 2.3 constant_dynamic-update-slice_fusion.6
  247.0 19.6 %constant_dynamic-update-slice_fusion.4 = bf16[4,256,11392]{2,1,0:T(8,128)(2,1)S(1)} fusion(bf16[4,256,11392]{2,1,0:T(8,128)(2,1)S(1)} %constant_dynamic-update-slice_fusion.5, f32[4,32,11392]{2,1,0:T(8,128)S(1)} %bitcast.39, f32[11392]{0:T(1024)S(1)} %fusion.4, f32[4,32]{1,0:T(4,128)S(1)} %constant_dynamic-slice_fusion.1, pred[11392]{0:T(1024)(128)(4,1)S(1)} %fusion.8), kind=kLoop, calls=%fused_computation.22 | loop fusion | flops 5832704 | bytes 8812544
  266.6 2.2 constant_dynamic-update-slice_fusion.3
  268.8 2.2 constant_dynamic-update-slice_fusion.2
  271.4 19.4 %constant_dynamic-update-slice_fusion = bf16[4,256,11392]{2,1,0:T(8,128)(2,1)S(1)} fusion(bf16[4,256,11392]{2,1,0:T(8,128)(2,1)S(1)} %constant_dynamic-update-slice_fusion.1, f32[4,32,11392]{2,1,0:T(8,128)S(1)} %bitcast.39, f32[11392]{0:T(1024)S(1)} %fusion.4, f32[4,32]{1,0:T(4,128)S(1)} %constant_dynamic-slice_fusion.1, pred[11392]{0:T(1024)(128)(4,1)S(1)} %fusion.8), kind=kLoop, calls=%fused_computation.18 | loop fusion | flops 5832704 | bytes 8812544 | tf_op jit(solution)/shard_map/jit(_roll_dynamic)/concatenate | solution.py:67
  290.8 0.9 constant_dynamic-slice_fusion
  291.8 4.4 %copy-done.2 = bf16[4,128,11392]{2,1,0:T(8,128)(2,1)} copy-done((bf16[4,128,11392]{2,1,0:T(8,128)(2,1)}, bf16[4,128,11392]{2,1,0:T(8,128)(2,1)S(1)}, u32[]{:S(2)}) %copy-start.2) | copy-done | bytes 11665432
  296.1 0.7 dynamic-slice_select_fusion
  296.9 0.6 dynamic_slice.23
  297.5 0.8 compare_reduce_fusion
  298.3 16.2 %copy.21 = bf16[11392,512]{1,0:T(8,128)(2,1)} copy(bf16[11392,512]{0,1:T(8,128)(2,1)} %bitcast.41) | data formatting | bytes 23330816 | tf_op jit(solution)/shard_map/dot_general | solution.py:24
  314.5 33.7 %all-reduce.2.cloned.1.call-done = bf16[512,128]{1,0:T(8,128)(2,1)} async-done(((bf16[512,128]{1,0:T(8,128)(2,1)}), bf16[512,128]{1,0:T(8,128)(2,1)}) %all-reduce.2.cloned.1.call-update) | async-done | bytes 131088 | tf_op jit(solution)/shard_map/psum | solution.py:70
  348.2 11.9 %fusion = f32[89,1,1,128,128]{4,3,2,1,0:T(8,128)} fusion(f32[89,1,1,128,128]{4,3,2,1,0:T(8,128)} %param.15, pred[89]{0:T(512)(128)(4,1)S(1)} %compare_reduce_fusion, bf16[89,128,512]{2,1,0:T(8,128)(2,1)} %bitcast.37, bf16[512,128]{1,0:T(8,128)(2,1)} %all-reduce.2.cloned.1.call-done, f32[512]{0:T(512)S(1)} %multiply_multiply_fusion), kind=kOutput, calls=%fused_computation.1 | convolution fusion | flops 1496285184 | bytes 23464024 | tf_op jit(solution)/shard_map/dot_general | solution.py:24
  (33 shorter events, 1.6 us)
Async XLA Ops:
  6.5 13.9 %copy-start = (f32[512]{0:T(512)S(1)}, f32[512]{0:T(512)}, u32[]{:S(2)}) copy-start(f32[512]{0:T(512)} %param.9) | copy-start | bytes 6148
  6.5 341.6 %all-reduce.2.cloned.1.call-start = ((), (), s32[]{:S(2)}) async-start(), calls=%async_computation | async-start | bytes 262144 | tf_op jit(solution)/shard_map/psum | solution.py:70
  20.4 156.6 %copy-start.3 = (s32[712]{0:T(1024)S(1)}, s32[712]{0:T(1024)}, u32[]{:S(2)}) copy-start(s32[712]{0:T(1024)} %param.13) | copy-start | bytes 8548
  20.4 160.3 %copy-start.5 = (s32[512]{0:T(512)S(1)}, s32[512]{0:T(512)}, u32[]{:S(2)}) copy-start(s32[512]{0:T(512)} %param.12) | copy-start | bytes 6148
  20.4 160.3 %copy-start.6 = (f32[8]{0:T(128)S(1)}, f32[8]{0:T(128)}, u32[]{:S(2)}) copy-start(f32[8]{0:T(128)} %param.11) | copy-start | bytes 100
  41.7 68.3 %collective-permute-start = (bf16[4,32,11392]{2,1,0:T(8,128)(2,1)S(1)}, bf16[4,32,11392]{2,1,0:T(8,128)(2,1)S(1)}, u32[]{:S(2)}, u32[]{:S(2)}) collective-permute-start(bf16[4,32,11392]{2,1,0:T(8,128)(2,1)S(1)} %select_convert_fusion), channel_id=1, source_target_pairs={{0,1},{1,2},{2,3},{3,0},{4,5},{5,6},{6,7},{7,4},{8,9},{9,10},{10,1... | collective-permute-start | bytes 8749064 | tf_op jit(solution)/shard_map/ppermute | solution.py:64
  110.1 66.3 %collective-permute-start.1 = (bf16[4,32,11392]{2,1,0:T(8,128)(2,1)S(1)}, bf16[4,32,11392]{2,1,0:T(8,128)(2,1)}, u32[]{:S(2)}, u32[]{:S(2)}) collective-permute-start(bf16[4,32,11392]{2,1,0:T(8,128)(2,1)S(1)} %collective-permute-done), channel_id=1, source_target_pairs={{0,1},{1,2},{2,3},{3,0},{4,5},{5,6},{6,7},{7,4},{8,9},{9,10},{10,1... | collective-permute-start | bytes 8749064 | tf_op jit(solution)/shard_map/ppermute | solution.py:64
  176.3 65.6 %collective-permute-start.2 = (bf16[4,32,11392]{2,1,0:T(8,128)(2,1)}, bf16[4,32,11392]{2,1,0:T(8,128)(2,1)}, u32[]{:S(2)}, u32[]{:S(2)}) collective-permute-start(bf16[4,32,11392]{2,1,0:T(8,128)(2,1)} %collective-permute-done.1), channel_id=1, source_target_pairs={{0,1},{1,2},{2,3},{3,0},{4,5},{5,6},{6,7},{7,4},{8,9},{9,10},{10,1... | collective-permute-start | bytes 8749064 | tf_op jit(solution)/shard_map/ppermute | solution.py:64
  241.9 5.0 %slice-start = ((s8[5832704]{0:T(1024)(128)(4,1)}), s8[4194304]{0:T(1024)(128)(4,1)S(1)}, s32[]{:S(2)}) async-start(s8[5832704]{0:T(1024)(128)(4,1)} %bitcast.38), calls=%async_computation.1 | async-start | bytes 8388608
  244.2 2.7 slice-start.1
  290.8 6.0 %copy-start.4 = (f32[512]{0:T(512)S(1)}, f32[512]{0:T(512)}, u32[]{:S(2)}) copy-start(f32[512]{0:T(512)} %param.10) | copy-start | bytes 6148
  291.8 4.4 %copy-start.2 = (bf16[4,128,11392]{2,1,0:T(8,128)(2,1)}, bf16[4,128,11392]{2,1,0:T(8,128)(2,1)S(1)}, u32[]{:S(2)}) copy-start(bf16[4,128,11392]{2,1,0:T(8,128)(2,1)S(1)} %constant_dynamic-slice_fusion) | copy-start | bytes 34996228
  348.2 11.9 %copy-start.1 = (f32[512]{0:T(512)S(1)}, f32[512]{0:T(512)}, u32[]{:S(2)}) copy-start(f32[512]{0:T(512)} %param.9) | copy-start | bytes 6148
Sparse Core Ops, SparseCore 0:
  297.0 51.1 all-reduce.1
